TPU v7x, 32 devices: a whole 2x2x4 slice. The times are simulated.
32 devices in a mesh: dp: 8 (over z, y), group: 4 (over x, core).
Axes of the slice: x: 2, y: 2, z: 4, core: 2. Of those that a mesh axis runs over, the one named last changes fastest.
Arguments:
- gradients: float32 [32, 3, 320, 960], P(('dp', 'group')), may hold values from -0.8 to 0.8
- errors: bfloat16 [32, 3, 320, 960], P(('dp', 'group')), may hold values from -0.59765625 to 0.59765625
- q_init: float32 [3, 960, 32], replicated, may hold values from -0.1875 to 0.1875
- owners: int32 [3], replicated, may hold values from 0 to 31, as said below
- buckets: int32 [3], replicated, may hold values from 0 to 3
- learn_rates: float32 [4], replicated, may hold values from 0.2 to 1
- beta_values: float32 [4], replicated, may hold values from 0.5 to 0.95
- momentum: bfloat16 [64, 320, 960], P(('dp', 'group')), may hold values from -3 to 3
Outputs:
- new_errors: bfloat16 [32, 3, 320, 960], P(('dp', 'group'))
- weight_steps: bfloat16 [32, 3, 320, 960], P(('dp', 'group'))
- new_momentum: bfloat16 [64, 320, 960], P(('dp', 'group'))
Inputs may be any that keep to these rules, and one draw needn't show every extreme that they name: `owners`: no device owns more than 2 matrices, and some device owns exactly 2.
All inputs are finite; a program needn't handle non-finite values.
Results may differ from a plain program's by a relative error of at most 0.001.
Values may be sent and summed in bfloat16 or wider, within the bound.
No kernel may reach another device: no remote copies, remote signals or barrier semaphores. Data moves between devices by JAX's collectives and lax.ppermute only.
A program may use at most 64 MiB of HBM per device.

v0:
```python
import jax
import jax.numpy as jnp
from jax import lax
from jax.sharding import PartitionSpec as P


def from_root(value, axis, source):
    kept = jnp.where(lax.axis_index(axis) == source, value, 0).astype(value.dtype)
    return lax.psum(kept, axis)


def on_device(gradients, errors, q_init, owners, buckets, learn_rates, beta_values, momentum):
    highest = lax.Precision.HIGHEST
    slot_count = momentum.shape[0]
    mat_count = owners.shape[0]
    bucket_count = learn_rates.shape[0]
    my_index = lax.axis_index(("dp", "group"))
    positions = jnp.arange(mat_count, dtype=jnp.int32)
    earlier = (owners[None, :] == owners[:, None]) & (positions[None, :] < positions[:, None])
    slot_list = jnp.sum(earlier.astype(jnp.int32), axis=1)
    bucket_hits = buckets[:, None] == jnp.arange(bucket_count, dtype=jnp.int32)[None, :]
    rate_list = jnp.sum(jnp.where(bucket_hits, learn_rates[None, :], 0.0), axis=1)
    beta_list = jnp.sum(jnp.where(bucket_hits, beta_values[None, :], 0.0), axis=1)
    merged = gradients[0] + errors[0].astype(jnp.float32)
    p_local = jnp.einsum("mkd,mdr->mkr", merged, q_init, precision=highest)
    p_sum = lax.psum(p_local, ("dp", "group"))
    gram_matrix = jnp.einsum("mkr,mks->mrs", p_sum, p_sum, precision=highest)
    lower_factor = jnp.linalg.cholesky(gram_matrix)
    p_hat = lax.linalg.triangular_solve(
        lower_factor, p_sum, left_side=False, lower=True, transpose_a=True
    )
    q_local = jnp.einsum("mkd,mkr->mdr", merged, p_hat, precision=highest)
    q_sum = lax.psum(q_local, ("dp", "group"))
    approx = jnp.einsum("mkr,mdr->mkd", p_hat, q_local, precision=highest)
    new_errors = (merged - approx).astype(jnp.bfloat16)
    update = jnp.einsum("mkr,mdr->mkd", p_hat, q_sum, precision=highest)
    slot_range = jnp.arange(slot_count, dtype=jnp.int32)
    new_slab = jnp.zeros(momentum.shape, jnp.float32)
    step_list = []
    for matrix in range(mat_count):
        old_state = lax.dynamic_index_in_dim(momentum, slot_list[matrix], 0, keepdims=False).astype(
            jnp.float32
        )
        mom_new = beta_list[matrix] * old_state + update[matrix]
        step_value = (-rate_list[matrix] * (update[matrix] + beta_list[matrix] * mom_new)).astype(
            jnp.bfloat16
        )
        step_value = from_root(step_value, ("dp", "group"), owners[matrix])
        step_list.append(step_value)
        selected = (slot_range == slot_list[matrix]) & (owners[matrix] == my_index)
        new_slab = new_slab + jnp.where(selected[:, None, None], mom_new[None], 0.0)
    return (new_errors[None], jnp.stack(step_list)[None], new_slab.astype(jnp.bfloat16))


def solution(mesh):
    placed = (
        P(("dp", "group"), None, None, None),
        P(("dp", "group"), None, None, None),
        P(),
        P(),
        P(),
        P(),
        P(),
        P(("dp", "group"), None, None),
    )
    return jax.shard_map(
        on_device,
        mesh=mesh,
        in_specs=placed,
        out_specs=(
            P(("dp", "group"), None, None, None),
            P(("dp", "group"), None, None, None),
            P(("dp", "group"), None, None),
        ),
        check_vma=False,
    )
```

profile of v0, /device:TPU:0, one launch (start us, length us, event | category | flops | bytes accessed | tf_op | source)
XLA Modules:
  0.0 456.5 jit_solution(16836187007871859211)
XLA Ops:
  7.2 0.9 copy-done
  8.2 7.3 %fusion.2 = f32[3,320,32]{1,2,0:T(8,128)} fusion(f32[3,960,32]{1,2,0:T(8,128)S(1)} %copy-done, f32[1,3,320,960]{3,2,1,0:T(8,128)} %param.8, bf16[1,3,320,960]{3,2,1,0:T(8,128)(2,1)} %param.9), kind=kOutput, calls=%fused_computation.3 | convolution fusion | flops 355737600 | bytes 6021120 | tf_op jit(solution)/shard_map/mkd,mdr->mkr/dot_general | solution.py:25
  15.7 0.7 fusion.28
  20.2 0.6 fusion.29
  24.7 114.3 %all-reduce.5.cloned.1.call-done = f32[3,320,32]{1,2,0:T(8,128)} async-done(((f32[3,320,32]{1,2,0:T(8,128)}), f32[3,320,32]{1,2,0:T(8,128)}) %all-reduce.5.cloned.1.call-update) | async-done | bytes 122896 | tf_op jit(solution)/shard_map/psum | solution.py:26
  139.0 1.3 fusion.32
  140.4 8.8 %custom-call.7 = f32[3,32,32]{2,1,0:T(8,128)S(1)} custom-call(f32[3,32,32]{2,1,0:T(8,128)S(1)} %fusion.26), custom_call_target="Cholesky" | custom-call | tf_op jit(solution)/shard_map/jit(cholesky)/cholesky | solution.py:28
  149.4 7.4 %custom-call.8 = f32[3,1,32,32]{2,3,1,0:T(8,128)S(1)} custom-call(f32[3,1,32,32]{3,2,1,0:T(8,128)S(1)} %select_bitcast_fusion), custom_call_target="InvertDiagBlocksLowerTriangular" | custom-call | tf_op jit(solution)/shard_map/triangular_solve | solution.py:29
  156.8 1.3 fusion.24
  158.1 4.8 %fusion = f32[3,960,32]{1,2,0:T(8,128)S(1)} fusion(f32[3,320,32]{1,2,0:T(8,128)S(1)} %fusion.24, f32[1,3,320,960]{3,2,1,0:T(8,128)} %param.8, bf16[1,3,320,960]{3,2,1,0:T(8,128)(2,1)S(1)} %copy-done.2), kind=kOutput, calls=%fused_computation.1 | convolution fusion | flops 355737600 | bytes 6021120 | tf_op jit(solution)/shard_map/mkd,mkr->mdr/dot_general | solution.py:32
  162.9 6.3 %fusion.5 = bf16[1,3,320,960]{3,2,1,0:T(8,128)(2,1)} fusion(f32[3,320,32]{1,2,0:T(8,128)S(1)} %fusion.24, f32[3,960,32]{1,2,0:T(8,128)S(1)} %fusion, f32[1,3,320,960]{3,2,1,0:T(8,128)} %param.8, bf16[1,3,320,960]{3,2,1,0:T(8,128)(2,1)S(1)} %copy-done.2), kind=kOutput, calls=%fused_computation.9 | convolution fusion | flops 357580800 | bytes 7864320 | tf_op jit(solution)/shard_map/mkr,mdr->mkd/dot_general | solution.py:34
  169.3 0.7 all-reduce.7.cloned.1.call-update
  170.0 0.2 all-reduce.9.cloned.1.call-start
  170.2 0.2 select_reduce_fusion.2
  170.4 0.7 fusion.30
  174.9 130.5 %all-reduce.7.cloned.1.call-done = f32[3,960,32]{1,2,0:T(8,128)} async-done(((f32[3,960,32]{1,2,0:T(8,128)}), f32[3,960,32]{1,2,0:T(8,128)}) %all-reduce.7.cloned.1.call-update) | async-done | bytes 368656 | tf_op jit(solution)/shard_map/psum | solution.py:33
  305.4 4.3 fusion.33
  309.7 3.9 fusion.19
  313.6 0.6 compare_and_fusion.2
  314.2 1.3 compare_and_fusion
  315.5 4.8 %add_bitcast_fusion.2 = (f32[320,960]{1,0:T(8,128)S(1)}, f32[320,960]{1,0:T(8,128)S(1)}, f32[320,960]{1,0:T(8,128)S(1)}) fusion(f32[3,320,960]{2,1,0:T(8,128)} %copy-done.1, f32[]{:T(128)} %bitcast.8, bf16[2,320,960]{2,1,0:T(8,128)(2,1)S(1)} %copy-done.3, s32[]{:T(128)S(6)} %select_n.55, s32[]{:T(128)S(6)} %select_n.58, f32[]{:T(128)} %bitcast.15, ...), kind=kLoop, calls=%fused_computation.27 | loop fusion | flops 2764800 | bytes 9216024 | tf_op jit(solution)/shard_map/jit(_where)/broadcast_in_dim | solution.py:51
  320.4 1.7 add_convert_fusion
  322.1 125.0 %all-reduce.9.cloned.1.call-done = (bf16[1,320,960]{2,1,0:T(8,128)(2,1)}, bf16[1,320,960]{2,1,0:T(8,128)(2,1)}, bf16[1,320,960]{2,1,0:T(8,128)(2,1)}) async-done(((bf16[1,320,960]{2,1,0:T(8,128)(2,1)}, bf16[1,320,960]{2,1,0:T(8,128)(2,1)}, bf16[1,320,960]{2,1,0:T(8,128)(2,1)}), (bf16[1,320,960]{2,1,0:T(8,128)(2,1)}, bf16[1,320,960]{2,1,0:T(8,128)(2,1)}, ...) | async-done | bytes 1843216 | tf_op jit(solution)/shard_map/psum | solution.py:9
  447.0 3.0 maximum_bitcast_fusion
  (29 shorter events, 0.6 us)
Async XLA Ops:
  7.2 1.0 copy-start
  7.2 8.3 %copy-start.5 = (s32[3]{0:T(128)S(1)}, s32[3]{0:T(128)}, u32[]{:S(2)}) copy-start(s32[3]{0:T(128)} %param.11) | copy-start | bytes 40
  7.2 131.8 %all-reduce.5.cloned.1.call-start = ((), (), s32[]{:S(2)}) async-start(), calls=%async_computation | async-start | bytes 294912 | tf_op jit(solution)/shard_map/psum | solution.py:26
  8.2 149.9 %copy-start.2 = (bf16[1,3,320,960]{3,2,1,0:T(8,128)(2,1)S(1)}, bf16[1,3,320,960]{3,2,1,0:T(8,128)(2,1)}, u32[]{:S(2)}) copy-start(bf16[1,3,320,960]{3,2,1,0:T(8,128)(2,1)} %param.9) | copy-start | bytes 5529604
  162.9 6.4 %copy-start.4 = (f32[3,960,32]{1,2,0:T(8,128)}, f32[3,960,32]{1,2,0:T(8,128)S(1)}, u32[]{:S(2)}) copy-start(f32[3,960,32]{1,2,0:T(8,128)S(1)} %fusion) | copy-start | bytes 1105924
  162.9 7.3 %copy-start.6 = (f32[4]{0:T(128)S(1)}, f32[4]{0:T(128)}, u32[]{:S(2)}) copy-start(f32[4]{0:T(128)} %param.13) | copy-start | bytes 52
  162.9 7.3 %copy-start.7 = (s32[3]{0:T(128)S(1)}, s32[3]{0:T(128)}, u32[]{:S(2)}) copy-start(s32[3]{0:T(128)} %param.12) | copy-start | bytes 40
  162.9 7.3 %copy-start.8 = (f32[4]{0:T(128)S(1)}, f32[4]{0:T(128)}, u32[]{:S(2)}) copy-start(f32[4]{0:T(128)} %param.14) | copy-start | bytes 52
  169.2 136.1 %all-reduce.7.cloned.1.call-start = ((), (), s32[]{:S(2)}) async-start(), calls=%async_computation.1 | async-start | bytes 786432 | tf_op jit(solution)/shard_map/psum | solution.py:33
  170.0 277.0 %all-reduce.9.cloned.1.call-start = ((), (), s32[]{:S(2)}) async-start(), calls=%async_computation.2 | async-start | bytes 3932160 | tf_op jit(solution)/shard_map/psum | solution.py:9
  174.9 134.8 %copy-start.3 = (bf16[2,320,960]{2,1,0:T(8,128)(2,1)S(1)}, bf16[2,320,960]{2,1,0:T(8,128)(2,1)}, u32[]{:S(2)}) copy-start(bf16[2,320,960]{2,1,0:T(8,128)(2,1)} %param.15) | copy-start | bytes 3686404
  309.7 3.9 copy-start.1
Sparse Core Ops, SparseCore 0:
  15.6 123.3 all-reduce.4
  175.9 129.3 all-reduce.6
  313.7 133.2 all-reduce.8
where the time goes:
time: 457 us
  waiting for transfers between devices  371 us (81%)
  other arithmetic  32.1 us (7%)
  between operations  25.4 us (6%)
  matrix products  25.2 us (6%)
    psum x1, waiting for transfers between devices, on_device(): q_sum = lax.psum(q_local, ('dp', 'group'))  131 us
    psum x1, waiting for transfers between devices, from_root(): return lax.psum(kept, axis)  125 us
    psum x1, waiting for transfers between devices, on_device(): p_sum = lax.psum(p_local, ('dp', 'group'))  114 us
  transfers between devices with their start and end apart: 3, of which 3 were waited for; matrix products, arithmetic and copies ran while one was open for 2% of the time, Pallas kernels for 0%

commit v1 on v0

--- a/solution.py
+++ b/solution.py
@@ -30,7 +30,9 @@
         lower_factor, p_sum, left_side=False, lower=True, transpose_a=True
     )
     q_local = jnp.einsum("mkd,mkr->mdr", merged, p_hat, precision=highest)
-    q_sum = lax.psum(q_local, ("dp", "group"))
+    q_sum = q_local
+    for name in ("group", "dp"):
+        q_sum = lax.psum(q_sum, name)
     approx = jnp.einsum("mkr,mdr->mkd", p_hat, q_local, precision=highest)
     new_errors = (merged - approx).astype(jnp.bfloat16)
     update = jnp.einsum("mkr,mdr->mkd", p_hat, q_sum, precision=highest)

time: 457 us -> 434 us (0.950)
  waiting for transfers between devices: 371 us -> 348 us
    psum x1 -> x2, waiting for transfers between devices: 131 us -> 98.5 us  [on_device(): q_sum = lax.psum(q_sum, name)]
    psum x1, waiting for transfers between devices: 114 us -> 123 us  [on_device(): p_sum = lax.psum(p_local, ('dp', 'group'))]
  transfers between devices with their start and end apart: 3 -> 4, of which waited for: 3 -> 4; matrix products, arithmetic and copies ran while one was open for 2% -> 2% of each run, Pallas kernels for 0% -> 0%
where the time goes in v1:
time: 434 us
  waiting for transfers between devices  348 us (80%)
  other arithmetic  32.1 us (7%)
  between operations  25.5 us (6%)
  matrix products  25.2 us (6%)
    psum x1, waiting for transfers between devices, from_root(): return lax.psum(kept, axis)  125 us
    psum x1, waiting for transfers between devices, on_device(): p_sum = lax.psum(p_local, ('dp', 'group'))  123 us
    psum x2, waiting for transfers between devices, on_device(): q_sum = lax.psum(q_sum, name)  98.5 us
    another operation x4, other arithmetic, on_device(): lower_factor = jnp.linalg.cholesky(gram_matrix)  8.96 us
  transfers between devices with their start and end apart: 4, of which 4 were waited for; matrix products, arithmetic and copies ran while one was open for 2% of the time, Pallas kernels for 0%

profile of v1, /device:TPU:0, one launch (start us, length us, event | category | flops | bytes accessed | tf_op | source)
XLA Modules:
  0.0 433.9 jit_solution(11584485724202148600)
XLA Ops:
  7.2 0.9 copy-done
  8.2 7.3 %fusion.2 = f32[3,320,32]{1,2,0:T(8,128)} fusion(f32[3,960,32]{1,2,0:T(8,128)S(1)} %copy-done, f32[1,3,320,960]{3,2,1,0:T(8,128)} %param.8, bf16[1,3,320,960]{3,2,1,0:T(8,128)(2,1)} %param.9), kind=kOutput, calls=%fused_computation.3 | convolution fusion | flops 355737600 | bytes 6021120 | tf_op jit(solution)/shard_map/mkd,mdr->mkr/dot_general | solution.py:25
  15.5 123.5 %all-reduce.6.cloned.1.call-done = f32[3,320,32]{1,2,0:T(8,128)} async-done(((f32[3,320,32]{1,2,0:T(8,128)}), f32[3,320,32]{1,2,0:T(8,128)}) %all-reduce.6.cloned.1.call-update) | async-done | bytes 122896 | tf_op jit(solution)/shard_map/psum | solution.py:26
  139.0 1.3 fusion.32
  140.4 8.8 %custom-call.7 = f32[3,32,32]{2,1,0:T(8,128)S(1)} custom-call(f32[3,32,32]{2,1,0:T(8,128)S(1)} %fusion.26), custom_call_target="Cholesky" | custom-call | tf_op jit(solution)/shard_map/jit(cholesky)/cholesky | solution.py:28
  149.4 7.4 %custom-call.8 = f32[3,1,32,32]{2,3,1,0:T(8,128)S(1)} custom-call(f32[3,1,32,32]{3,2,1,0:T(8,128)S(1)} %select_bitcast_fusion), custom_call_target="InvertDiagBlocksLowerTriangular" | custom-call | tf_op jit(solution)/shard_map/triangular_solve | solution.py:29
  156.8 1.3 fusion.24
  158.1 4.8 %fusion = f32[3,960,32]{1,2,0:T(8,128)S(1)} fusion(f32[3,320,32]{1,2,0:T(8,128)S(1)} %fusion.24, f32[1,3,320,960]{3,2,1,0:T(8,128)} %param.8, bf16[1,3,320,960]{3,2,1,0:T(8,128)(2,1)S(1)} %copy-done.2), kind=kOutput, calls=%fused_computation.1 | convolution fusion | flops 355737600 | bytes 6021120 | tf_op jit(solution)/shard_map/mkd,mkr->mdr/dot_general | solution.py:32
  162.9 6.3 %fusion.5 = bf16[1,3,320,960]{3,2,1,0:T(8,128)(2,1)} fusion(f32[3,320,32]{1,2,0:T(8,128)S(1)} %fusion.24, f32[3,960,32]{1,2,0:T(8,128)S(1)} %fusion, f32[1,3,320,960]{3,2,1,0:T(8,128)} %param.8, bf16[1,3,320,960]{3,2,1,0:T(8,128)(2,1)S(1)} %copy-done.2), kind=kOutput, calls=%fused_computation.9 | convolution fusion | flops 357580800 | bytes 7864320 | tf_op jit(solution)/shard_map/mkr,mdr->mkd/dot_general | solution.py:36
  169.3 0.7 all-reduce.8.cloned.1.call-update
  170.2 37.4 %all-reduce.8.cloned.1.call-done = f32[3,960,32]{1,2,0:T(8,128)} async-done(((f32[3,960,32]{1,2,0:T(8,128)}), f32[3,960,32]{1,2,0:T(8,128)}) %all-reduce.8.cloned.1.call-update) | async-done | bytes 368656 | tf_op jit(solution)/shard_map/psum | solution.py:35
  207.6 0.2 all-reduce.12.cloned.1.call-start
  207.8 0.7 fusion.28
  212.3 0.6 fusion.29
  217.0 0.7 fusion.30
  221.6 61.2 %all-reduce.10.cloned.1.call-done = f32[3,960,32]{1,2,0:T(8,128)} async-done(((f32[3,960,32]{1,2,0:T(8,128)}), f32[3,960,32]{1,2,0:T(8,128)}) %all-reduce.10.cloned.1.call-update) | async-done | bytes 368656 | tf_op jit(solution)/shard_map/psum | solution.py:35
  282.7 4.3 fusion.33
  287.0 3.9 fusion.19
  290.9 0.6 compare_and_fusion.2
  291.6 1.3 compare_and_fusion
  292.9 4.8 %add_bitcast_fusion.2 = (f32[320,960]{1,0:T(8,128)S(1)}, f32[320,960]{1,0:T(8,128)S(1)}, f32[320,960]{1,0:T(8,128)S(1)}) fusion(f32[3,320,960]{2,1,0:T(8,128)} %copy-done.1, f32[]{:T(128)} %bitcast.8, bf16[2,320,960]{2,1,0:T(8,128)(2,1)S(1)} %copy-done.3, s32[]{:T(128)S(6)} %select_n.55, s32[]{:T(128)S(6)} %select_n.58, f32[]{:T(128)} %bitcast.15, ...), kind=kLoop, calls=%fused_computation.27 | loop fusion | flops 2764800 | bytes 9216024 | tf_op jit(solution)/shard_map/jit(_where)/broadcast_in_dim | solution.py:53
  297.7 1.7 add_convert_fusion
  299.4 125.0 %all-reduce.12.cloned.1.call-done = (bf16[1,320,960]{2,1,0:T(8,128)(2,1)}, bf16[1,320,960]{2,1,0:T(8,128)(2,1)}, bf16[1,320,960]{2,1,0:T(8,128)(2,1)}) async-done(((bf16[1,320,960]{2,1,0:T(8,128)(2,1)}, bf16[1,320,960]{2,1,0:T(8,128)(2,1)}, bf16[1,320,960]{2,1,0:T(8,128)(2,1)}), (bf16[1,320,960]{2,1,0:T(8,128)(2,1)}, bf16[1,320,960]{2,1,0:T(8,128)(2,1)}, ...) | async-done | bytes 1843216 | tf_op jit(solution)/shard_map/psum | solution.py:9
  424.4 3.0 maximum_bitcast_fusion
  (32 shorter events, 0.9 us)
Async XLA Ops:
  7.2 1.0 copy-start
  7.2 131.8 %all-reduce.6.cloned.1.call-start = ((), (), s32[]{:S(2)}) async-start(), calls=%async_computation | async-start | bytes 294912 | tf_op jit(solution)/shard_map/psum | solution.py:26
  8.2 149.9 %copy-start.2 = (bf16[1,3,320,960]{3,2,1,0:T(8,128)(2,1)S(1)}, bf16[1,3,320,960]{3,2,1,0:T(8,128)(2,1)}, u32[]{:S(2)}) copy-start(bf16[1,3,320,960]{3,2,1,0:T(8,128)(2,1)} %param.9) | copy-start | bytes 5529604
  162.9 6.4 %copy-start.4 = (f32[3,960,32]{1,2,0:T(8,128)}, f32[3,960,32]{1,2,0:T(8,128)S(1)}, u32[]{:S(2)}) copy-start(f32[3,960,32]{1,2,0:T(8,128)S(1)} %fusion) | copy-start | bytes 1105924
  162.9 7.2 %copy-start.5 = (s32[3]{0:T(128)S(1)}, s32[3]{0:T(128)}, u32[]{:S(2)}) copy-start(s32[3]{0:T(128)} %param.11) | copy-start | bytes 40
  162.9 53.9 %copy-start.6 = (f32[4]{0:T(128)S(1)}, f32[4]{0:T(128)}, u32[]{:S(2)}) copy-start(f32[4]{0:T(128)} %param.13) | copy-start | bytes 52
  162.9 53.9 %copy-start.7 = (s32[3]{0:T(128)S(1)}, s32[3]{0:T(128)}, u32[]{:S(2)}) copy-start(s32[3]{0:T(128)} %param.12) | copy-start | bytes 40
  162.9 53.9 %copy-start.8 = (f32[4]{0:T(128)S(1)}, f32[4]{0:T(128)}, u32[]{:S(2)}) copy-start(f32[4]{0:T(128)} %param.14) | copy-start | bytes 52
  169.3 38.3 %all-reduce.8.cloned.1.call-start = ((), (), s32[]{:S(2)}) async-start(), calls=%async_computation.1 | async-start | bytes 786432 | tf_op jit(solution)/shard_map/psum | solution.py:35
  170.0 112.7 %all-reduce.10.cloned.1.call-start = ((), (), s32[]{:S(2)}) async-start(), calls=%async_computation.2 | async-start | bytes 786432 | tf_op jit(solution)/shard_map/psum | solution.py:35
  207.6 216.8 %all-reduce.12.cloned.1.call-start = ((), (), s32[]{:S(2)}) async-start(), calls=%async_computation.3 | async-start | bytes 3932160 | tf_op jit(solution)/shard_map/psum | solution.py:9
  221.5 65.5 %copy-start.3 = (bf16[2,320,960]{2,1,0:T(8,128)(2,1)S(1)}, bf16[2,320,960]{2,1,0:T(8,128)(2,1)}, u32[]{:S(2)}) copy-start(bf16[2,320,960]{2,1,0:T(8,128)(2,1)} %param.15) | copy-start | bytes 3686404
  287.0 3.9 copy-start.1
Sparse Core Ops, SparseCore 0:
  15.6 123.3 all-reduce.5
  173.0 34.5 all-reduce.7
  211.3 71.3 all-reduce.9
  291.1 133.3 all-reduce.11
